TPU v7x, 32 devices: a whole 2x2x4 slice. The times are simulated.
32 devices in a mesh: section: 4 (over z), tensor: 8 (over y, x, core).
Axes of the slice: x: 2, y: 2, z: 4, core: 2. Of those that a mesh axis runs over, the one named last changes fastest.
Arguments:
- resid: bfloat16 [32, 3584], P('tensor'), may hold values from -6 to 6
- w_enc: bfloat16 [7168, 3584], P(('section', 'tensor')), may hold values from -0.09375 to 0.09375
- b_enc: float32 [7168], P(('section', 'tensor')), may hold values from -1 to 0.5
- w_dec: bfloat16 [7168, 3584], P(('section', 'tensor')), may hold values from -0.0625 to 0.0625
- b_dec: float32 [3584], replicated, may hold values from -3 to 3
Outputs:
- recon: float32 [32, 3584], P('tensor')
- grad_w_dec: bfloat16 [7168, 3584], P(('section', 'tensor'))
- code_grad: float32 [32, 7168], P(None, ('section', 'tensor'))
- grad_b_dec: float32 [3584], replicated
- loss_value: float32 [], replicated
All inputs are finite; a program needn't handle non-finite values.
Results may differ from a plain program's by a relative error of at most 0.0032.
The roundings to bfloat16 on the way count: a program that leaves them out, or rounds other values in their place, can miss the bound.
Values may be sent and summed in bfloat16 or wider, within the bound.
No kernel may reach another device: no remote copies, remote signals or barrier semaphores. Data moves between devices by JAX's collectives and lax.ppermute only.
A program may use at most 64 MiB of HBM per device.

v0:
```python
import jax
import jax.numpy as jnp
from jax import lax
from jax.sharding import PartitionSpec as P

epsilon = 1e-06


def per_device(resid, w_enc, b_enc, w_dec, b_dec):
    stream = lax.all_gather(resid, "tensor", axis=0, tiled=True)
    preact = (
        lax.dot_general(stream, w_enc, (((1,), (1,)), ((), ())), preferred_element_type=jnp.float32)
        + b_enc
    )
    codes = jnp.maximum(preact, 0.0).astype(jnp.bfloat16)
    codes_f32 = codes.astype(jnp.float32)
    dec_f32 = w_dec.astype(jnp.float32)
    dec_norm = jnp.sqrt(jnp.sum(dec_f32 * dec_f32, axis=1) + epsilon)
    penalty = lax.psum(jnp.sum(codes_f32 * dec_norm), ("section", "tensor"))
    total_rows = stream.shape[0]
    model_width = stream.shape[1]
    shares = lax.psum_scatter(
        jnp.dot(codes, w_dec, preferred_element_type=jnp.float32),
        "tensor",
        scatter_dimension=0,
        tiled=True,
    )
    shares = lax.psum(shares, "section")
    recon = shares + b_dec
    errors = recon - resid.astype(jnp.float32)
    squares, grad_b_dec = lax.psum((jnp.sum(errors * errors), jnp.sum(errors, axis=0)), "tensor")
    err_half = lax.all_gather(errors.astype(jnp.bfloat16), "tensor", axis=0, tiled=True)
    loss_value = (0.5 * squares + penalty) / (total_rows * model_width)
    code_sums = jnp.sum(codes_f32, axis=0)
    grad_w_dec = lax.dot_general(
        codes, err_half, (((0,), (0,)), ((), ())), preferred_element_type=jnp.float32
    )
    grad_w_dec = grad_w_dec + code_sums[:, None] * dec_f32 / dec_norm[:, None]
    code_grad = (
        lax.dot_general(
            err_half, w_dec, (((1,), (1,)), ((), ())), preferred_element_type=jnp.float32
        )
        + dec_norm
    )
    return (recon, grad_w_dec.astype(jnp.bfloat16), code_grad, grad_b_dec, loss_value)


def solution(mesh):
    in_specs = (
        P("tensor", None),
        P(("section", "tensor"), None),
        P(("section", "tensor")),
        P(("section", "tensor"), None),
        P(),
    )
    out_specs = (
        P("tensor", None),
        P(("section", "tensor"), None),
        P(None, ("section", "tensor")),
        P(),
        P(),
    )
    return jax.shard_map(
        per_device, mesh=mesh, in_specs=in_specs, out_specs=out_specs, check_vma=False
    )
```

profile of v0, /device:TPU:0, one launch (start us, length us, event | category | flops | bytes accessed | tf_op | source)
XLA Modules:
  0.0 148.7 jit_solution(17115211651597049739)
XLA Ops:
  7.2 0.0 copy-start
  7.2 0.0 copy-start.2
  7.2 0.0 copy-start.6
  7.2 0.0 all-reduce.4.cloned.1.call-start
  7.2 1.9 %fusion.2 = f32[224]{0:T(256)S(1)} fusion(bf16[224,3584]{1,0:T(8,128)(2,1)} %param.8), kind=kLoop, calls=%fused_computation.5 | loop fusion | flops 2408224 | bytes 1606528 | tf_op jit(solution)/shard_map/reduce_sum | solution.py:18
  9.2 0.0 copy-start.1
  9.2 0.0 copy-done.2
  9.2 12.0 %all-gather = bf16[8,4,3584]{2,1,0:T(4,128)(2,1)} all-gather(bf16[1,4,3584]{2,1,0:T(4,128)(2,1)S(1)} %bitcast.12), channel_id=1, replica_groups=mesh['section'=4,'tensor'=8] {'tensor'}, dimensions={0}, use_global_device_ids=true | all-gather | bytes 258048 | tf_op jit(solution)/shard_map/all_gather | solution.py:10
  21.2 1.0 reshape.22
  22.2 0.0 copy-done
  22.2 0.0 copy-done.6
  22.2 1.2 fusion.5
  23.4 0.0 copy-start.7
  23.4 0.0 copy-start.5
  23.4 0.0 copy-done.1
  23.4 1.2 fusion.7
  24.5 0.0 all-reduce.4.cloned.1.call-update
  24.5 39.9 %psum.31 = f32[]{:T(128)} all-reduce(f32[]{:T(128)} %get-tuple-element.7), channel_id=1, replica_groups=mesh['section'=4,'tensor'=8] {'section','tensor'}, use_global_device_ids=true, to_apply=%region_9.0 | all-reduce | flops 1 | bytes 8 | tf_op jit(solution)/shard_map/psum | solution.py:19
  64.4 0.0 copy-done.7
  64.4 0.6 dynamic-slice
  65.7 14.0 %all-reduce.4.cloned.1.call-done = f32[32,3584]{1,0:T(8,128)} async-done(((f32[32,3584]{1,0:T(8,128)}), f32[32,3584]{1,0:T(8,128)}) %all-reduce.4.cloned.1.call-update) | async-done | bytes 458768
  79.7 0.9 constant_dynamic-slice_fusion
  80.6 19.6 %psum.28 = f32[4,3584]{1,0:T(4,128)S(1)} all-reduce(f32[4,3584]{1,0:T(4,128)S(1)} %constant_dynamic-slice_fusion), channel_id=1, replica_groups=mesh['section'=4,'tensor'=8] {'section'}, use_global_device_ids=true, to_apply=%region_1.0 | all-reduce | flops 14336 | bytes 114688 | tf_op jit(solution)/shard_map/psum | solution.py:28
  100.2 0.0 copy-done.5
  100.2 0.7 multiply_reduce_fusion
  100.9 0.0 copy-start.3
  101.0 9.6 %all-gather.1 = bf16[8,4,3584]{2,1,0:T(4,128)(2,1)} all-gather(bf16[1,4,3584]{2,1,0:T(4,128)(2,1)S(1)} %convert_bitcast_fusion), channel_id=1, replica_groups=mesh['section'=4,'tensor'=8] {'tensor'}, dimensions={0}, use_global_device_ids=true | all-gather | bytes 258048 | tf_op jit(solution)/shard_map/all_gather | solution.py:32
  110.6 1.0 reshape.24
  111.6 1.2 convolution_add_fusion.1
  112.8 0.0 copy-start.4
  112.8 1.8 %fusion = bf16[224,3584]{1,0:T(8,128)(2,1)} fusion(bf16[32,224]{1,0:T(8,128)(2,1)S(1)} %get-tuple-element.12, bf16[32,3584]{1,0:T(8,128)(2,1)S(1)} %reshape.24, bf16[224,3584]{1,0:T(8,128)(2,1)S(1)} %copy-done.1, f32[224]{0:T(256)S(1)} %add_sqrt_fusion, f32[224]{0:T(256)S(1)} %get-tuple-element.8), kind=kOutput, calls=%fused_computation.1 | convolution fusion | flops 55394304 | bytes 3456768 | tf_op jit(solution)/shard_map/dot_general | solution.py:35
  114.6 0.0 copy-done.3
  114.6 0.0 copy-done.4
  114.6 24.8 %all-reduce.1 = (f32[3584]{0:T(1024)}, f32[]{:T(128)}) all-reduce(f32[3584]{0:T(1024)S(1)} %copy-done.4, f32[]{:T(128)} %get-tuple-element.5), channel_id=1, replica_groups=mesh['section'=4,'tensor'=8] {'tensor'}, use_global_device_ids=true, to_apply=%region_5.0 | all-reduce | flops 3585 | bytes 28680 | tf_op jit(solution)/shard_map/psum | solution.py:31
  (2 shorter events, 0.0 us)
Async XLA Ops:
  7.2 15.0 %copy-start = (bf16[224,3584]{1,0:T(8,128)(2,1)S(1)}, bf16[224,3584]{1,0:T(8,128)(2,1)}, u32[]{:S(2)}) copy-start(bf16[224,3584]{1,0:T(8,128)(2,1)} %param.6) | copy-start | bytes 4816900
  7.2 2.0 %copy-start.2 = (bf16[4,3584]{1,0:T(4,128)(2,1)S(1)}, bf16[4,3584]{1,0:T(4,128)(2,1)}, u32[]{:S(2)}) copy-start(bf16[4,3584]{1,0:T(4,128)(2,1)} %param.5) | copy-start | bytes 86020
  7.2 15.0 %copy-start.6 = (f32[224]{0:T(256)S(1)}, f32[224]{0:T(256)}, u32[]{:S(2)}) copy-start(f32[224]{0:T(256)} %param.7) | copy-start | bytes 2692
  7.2 72.5 %all-reduce.4.cloned.1.call-start = ((), (), s32[]{:S(2)}) async-start(), calls=%async_computation | async-start | bytes 917504
  9.2 14.2 %copy-start.1 = (bf16[224,3584]{1,0:T(8,128)(2,1)S(1)}, bf16[224,3584]{1,0:T(8,128)(2,1)}, u32[]{:S(2)}) copy-start(bf16[224,3584]{1,0:T(8,128)(2,1)} %param.8) | copy-start | bytes 4816900
  23.4 41.1 %copy-start.7 = (u32[32]{0:T(128)S(1)}, u32[32]{0:T(128)}, u32[]{:S(2)}) copy-start(u32[32]{0:T(128)} %constant.13) | copy-start | bytes 388
  23.4 76.8 %copy-start.5 = (f32[3584]{0:T(1024)S(1)}, f32[3584]{0:T(1024)}, u32[]{:S(2)}) copy-start(f32[3584]{0:T(1024)} %param.9) | copy-start | bytes 43012
  100.9 13.6 %copy-start.3 = (f32[4,3584]{1,0:T(4,128)}, f32[4,3584]{1,0:T(4,128)S(1)}, u32[]{:S(2)}) copy-start(f32[4,3584]{1,0:T(4,128)S(1)} %get-tuple-element.11) | copy-start | bytes 172036
  112.8 1.8 %copy-start.4 = (f32[3584]{0:T(1024)S(1)}, f32[3584]{0:T(1024)}, u32[]{:S(2)}) copy-start(f32[3584]{0:T(1024)} %get-tuple-element.6) | copy-start | bytes 43012
Sparse Core Ops, SparseCore 0:
  24.7 54.9 all-reduce.3
where the time goes:
time: 149 us
  blocking collectives  106 us (71%)
  between operations  17.2 us (12%)
  waiting for transfers between devices  14 us (9%)
  matrix products  5.33 us (4%)
  local copies, waits for them, and re-layouts  3.52 us (2%)
  other arithmetic  2.7 us (2%)
    psum x1, blocking collectives, per_device(): penalty = lax.psum(jnp.sum(codes_f32 * dec_norm), ('section', 'tensor'))  39.9 us
    psum x1, blocking collectives, per_device(): lax.psum((jnp.sum(errors * errors), jnp.sum(errors, axis=0)), 'tensor')  24.8 us
    psum x1, blocking collectives, per_device(): shares = lax.psum(shares, 'section')  19.6 us
    unnamed x2, waiting for transfers between devices  14 us
    all_gather x1, blocking collectives, per_device(): stream = lax.all_gather(resid, 'tensor', axis=0, tiled=True)  12 us
    all_gather x1, blocking collectives, per_device(): lax.all_gather(errors.astype(jnp.bfloat16), 'tensor', axis=0, tiled=True)  9.61 us
    unnamed x20, local copies, waits for them, and re-layouts  3.52 us
  transfers between devices with their start and end apart: 1, of which 1 were waited for; matrix products, arithmetic and copies ran while one was open for 0% of the time, Pallas kernels for 0%

commit v1 on v0

--- a/solution.py
+++ b/solution.py
@@ -7,7 +7,17 @@
 
 
 def per_device(resid, w_enc, b_enc, w_dec, b_dec):
-    stream = lax.all_gather(resid, "tensor", axis=0, tiled=True)
+    size_here = lax.axis_size("tensor")
+    mid_arr = resid
+    history = [mid_arr]
+    before = sorted(((k, (k + 1) % size_here) for k in range(size_here)))
+    for dd in range(1, size_here):
+        mid_arr = lax.ppermute(mid_arr, "tensor", before)
+        history.insert(0, mid_arr)
+    y = jnp.concatenate(history, 0)
+    answer = lax.axis_index("tensor")
+    taken_in = answer + 1
+    stream = jnp.roll(y, taken_in * resid.shape[0], 0)
     preact = (
         lax.dot_general(stream, w_enc, (((1,), (1,)), ((), ())), preferred_element_type=jnp.float32)
         + b_enc

time: 149 us -> 171 us (1.15)
  waiting for transfers between devices: 14 us -> 42 us
  blocking collectives: 106 us -> 94.5 us
  local copies, waits for them, and re-layouts: 3.52 us -> 7.85 us
    ppermute x0 -> x7, waiting for transfers between devices: none -> 27.9 us  [per_device(): mid_arr = lax.ppermute(mid_arr, 'tensor', before)]
    all_gather x1 -> x0, blocking collectives: 12 us -> none  [per_device(): stream = lax.all_gather(resid, 'tensor', axis=0, tiled=True)]
    concatenate x0 -> x1, local copies, waits for them, and re-layouts: none -> 5.32 us  [per_device(): stream = jnp.roll(y, taken_in * resid.shape[0], 0)]
    unnamed x20 -> x17, local copies, waits for them, and re-layouts: 3.52 us -> 2.52 us
  transfers between devices with their start and end apart: 1 -> 8, of which waited for: 1 -> 8; matrix products, arithmetic and copies ran while one was open for 0% -> 1% of each run, Pallas kernels for 0% -> 0%
where the time goes in v1:
time: 171 us
  blocking collectives  94.5 us (55%)
  waiting for transfers between devices  42 us (25%)
  between operations  17.2 us (10%)
  local copies, waits for them, and re-layouts  7.85 us (5%)
  matrix products  6.28 us (4%)
  other arithmetic  2.49 us (1%)
    psum x1, blocking collectives, per_device(): penalty = lax.psum(jnp.sum(codes_f32 * dec_norm), ('section', 'tensor'))  40.5 us
    ppermute x7, waiting for transfers between devices, per_device(): mid_arr = lax.ppermute(mid_arr, 'tensor', before)  27.9 us
    psum x1, blocking collectives, per_device(): lax.psum((jnp.sum(errors * errors), jnp.sum(errors, axis=0)), 'tensor')  24.8 us
    psum x1, blocking collectives, per_device(): shares = lax.psum(shares, 'section')  19.6 us
    unnamed x2, waiting for transfers between devices  14.1 us
    all_gather x1, blocking collectives, per_device(): lax.all_gather(errors.astype(jnp.bfloat16), 'tensor', axis=0, tiled=True)  9.61 us
    concatenate x1, local copies, waits for them, and re-layouts, per_device(): stream = jnp.roll(y, taken_in * resid.shape[0], 0)  5.32 us
  transfers between devices with their start and end apart: 8, of which 8 were waited for; matrix products, arithmetic and copies ran while one was open for 1% of the time, Pallas kernels for 0%

profile of v1, /device:TPU:0, one launch (start us, length us, event | category | flops | bytes accessed | tf_op | source)
XLA Modules:
  0.0 171.0 jit_solution(4529813834119935268)
XLA Ops:
  7.2 0.0 copy-start
  7.2 0.0 copy-start.2
  7.2 0.0 copy-start.5
  7.2 0.0 all-reduce.4.cloned.1.call-start
  7.2 0.5 collective-permute-start
  7.8 4.6 %collective-permute-done = bf16[4,3584]{1,0:T(4,128)(2,1)S(1)} collective-permute-done((bf16[4,3584]{1,0:T(4,128)(2,1)}, bf16[4,3584]{1,0:T(4,128)(2,1)S(1)}, u32[]{:S(2)}, u32[]{:S(2)}) %collective-permute-start) | collective-permute-done | bytes 28704 | tf_op jit(solution)/shard_map/ppermute | solution.py:15
  12.4 0.0 collective-permute-start.1
  12.4 4.2 %collective-permute-done.1 = bf16[4,3584]{1,0:T(4,128)(2,1)S(1)} collective-permute-done((bf16[4,3584]{1,0:T(4,128)(2,1)S(1)}, bf16[4,3584]{1,0:T(4,128)(2,1)S(1)}, u32[]{:S(2)}, u32[]{:S(2)}) %collective-permute-start.1) | collective-permute-done | bytes 28704 | tf_op jit(solution)/shard_map/ppermute | solution.py:15
  16.6 0.0 collective-permute-start.2
  16.6 4.2 %collective-permute-done.2 = bf16[4,3584]{1,0:T(4,128)(2,1)S(1)} collective-permute-done((bf16[4,3584]{1,0:T(4,128)(2,1)S(1)}, bf16[4,3584]{1,0:T(4,128)(2,1)S(1)}, u32[]{:S(2)}, u32[]{:S(2)}) %collective-permute-start.2) | collective-permute-done | bytes 28704 | tf_op jit(solution)/shard_map/ppermute | solution.py:15
  20.8 0.0 collective-permute-start.3
  20.8 4.2 %collective-permute-done.3 = bf16[4,3584]{1,0:T(4,128)(2,1)S(1)} collective-permute-done((bf16[4,3584]{1,0:T(4,128)(2,1)S(1)}, bf16[4,3584]{1,0:T(4,128)(2,1)S(1)}, u32[]{:S(2)}, u32[]{:S(2)}) %collective-permute-start.3) | collective-permute-done | bytes 28704 | tf_op jit(solution)/shard_map/ppermute | solution.py:15
  25.0 0.0 collective-permute-start.4
  25.0 4.2 %collective-permute-done.4 = bf16[4,3584]{1,0:T(4,128)(2,1)S(1)} collective-permute-done((bf16[4,3584]{1,0:T(4,128)(2,1)S(1)}, bf16[4,3584]{1,0:T(4,128)(2,1)S(1)}, u32[]{:S(2)}, u32[]{:S(2)}) %collective-permute-start.4) | collective-permute-done | bytes 28704 | tf_op jit(solution)/shard_map/ppermute | solution.py:15
  29.2 0.0 collective-permute-start.5
  29.2 1.8 %fusion.2 = f32[224]{0:T(256)S(1)} fusion(bf16[224,3584]{1,0:T(8,128)(2,1)} %param.8), kind=kLoop, calls=%fused_computation.5 | loop fusion | flops 2408224 | bytes 1606528 | tf_op jit(solution)/shard_map/reduce_sum | solution.py:28
  31.0 0.0 copy-start.1
  31.0 2.4 %collective-permute-done.5 = bf16[4,3584]{1,0:T(4,128)(2,1)S(1)} collective-permute-done((bf16[4,3584]{1,0:T(4,128)(2,1)S(1)}, bf16[4,3584]{1,0:T(4,128)(2,1)S(1)}, u32[]{:S(2)}, u32[]{:S(2)}) %collective-permute-start.5) | collective-permute-done | bytes 28704 | tf_op jit(solution)/shard_map/ppermute | solution.py:15
  33.4 0.0 collective-permute-start.6
  33.4 4.2 %collective-permute-done.6 = bf16[4,3584]{1,0:T(4,128)(2,1)S(1)} collective-permute-done((bf16[4,3584]{1,0:T(4,128)(2,1)S(1)}, bf16[4,3584]{1,0:T(4,128)(2,1)S(1)}, u32[]{:S(2)}, u32[]{:S(2)}) %collective-permute-start.6) | collective-permute-done | bytes 28704 | tf_op jit(solution)/shard_map/ppermute | solution.py:15
  37.6 0.0 copy-done.2
  37.6 5.3 %concatenate.6 = bf16[64,3584]{1,0:T(8,128)(2,1)} concatenate(bf16[4,3584]{1,0:T(4,128)(2,1)S(1)} %collective-permute-done.6, bf16[4,3584]{1,0:T(4,128)(2,1)S(1)} %collective-permute-done.5, bf16[4,3584]{1,0:T(4,128)(2,1)S(1)} %collective-permute-done.4, bf16[4,3584]{1,0:T(4,128)(2,1)S(1)} %collective-permute-done.3, bf16[4,3584]{1,0:T(4,128)(2,1)S(1)} %collective-permute-done.2, ...), dimensions={0} | concatenate | bytes 917504 | tf_op jit(solution)/shard_map/jit(_roll_dynamic)/concatenate | solution.py:20
  42.9 0.0 copy-done
  42.9 0.0 copy-done.5
  42.9 2.1 %fusion.6 = (f32[]{:T(128)}, f32[224]{0:T(256)S(1)}, bf16[32,224]{1,0:T(8,128)(2,1)S(1)}) fusion(f32[224]{0:T(256)S(1)} %add_sqrt_fusion, f32[224]{0:T(256)S(1)} %copy-done.5, bf16[224,3584]{1,0:T(8,128)(2,1)S(1)} %copy-done, bf16[64,3584]{1,0:T(8,128)(2,1)} %concatenate.6, s32[]{:T(128)S(6)} %select_n.14), kind=kOutput, calls=%fused_computation.15 | convolution fusion | flops 51430176 | bytes 1852040 | tf_op jit(solution)/shard_map/dot_general | solution.py:22
  45.1 0.0 copy-start.6
  45.1 0.0 copy-start.4
  45.1 0.0 copy-done.1
  45.1 1.2 fusion.9
  46.2 0.0 all-reduce.4.cloned.1.call-update
  46.3 0.0 copy-done.6
  46.3 0.6 dynamic-slice
  47.5 40.5 %psum.31 = f32[]{:T(128)} all-reduce(f32[]{:T(128)} %get-tuple-element.7), channel_id=1, replica_groups=mesh['section'=4,'tensor'=8] {'section','tensor'}, use_global_device_ids=true, to_apply=%region_9.10 | all-reduce | flops 1 | bytes 8 | tf_op jit(solution)/shard_map/psum | solution.py:29
  88.1 14.1 %all-reduce.4.cloned.1.call-done = f32[32,3584]{1,0:T(8,128)} async-done(((f32[32,3584]{1,0:T(8,128)}), f32[32,3584]{1,0:T(8,128)}) %all-reduce.4.cloned.1.call-update) | async-done | bytes 458768
  102.2 0.9 constant_dynamic-slice_fusion
  103.1 19.6 %psum.28 = f32[4,3584]{1,0:T(4,128)S(1)} all-reduce(f32[4,3584]{1,0:T(4,128)S(1)} %constant_dynamic-slice_fusion), channel_id=1, replica_groups=mesh['section'=4,'tensor'=8] {'section'}, use_global_device_ids=true, to_apply=%region_1.2 | all-reduce | flops 14336 | bytes 114688 | tf_op jit(solution)/shard_map/psum | solution.py:38
  122.6 0.0 copy-done.4
  122.7 0.7 multiply_reduce_fusion
  123.3 0.0 copy-start.3
  123.3 9.6 %all-gather = bf16[8,4,3584]{2,1,0:T(4,128)(2,1)} all-gather(bf16[1,4,3584]{2,1,0:T(4,128)(2,1)S(1)} %convert_bitcast_fusion), channel_id=1, replica_groups=mesh['section'=4,'tensor'=8] {'tensor'}, dimensions={0}, use_global_device_ids=true | all-gather | bytes 258048 | tf_op jit(solution)/shard_map/all_gather | solution.py:42
  132.9 1.0 reshape.22
  133.9 1.2 convolution_add_fusion.1
  135.1 1.8 %fusion = bf16[224,3584]{1,0:T(8,128)(2,1)} fusion(bf16[32,224]{1,0:T(8,128)(2,1)S(1)} %get-tuple-element.12, bf16[32,3584]{1,0:T(8,128)(2,1)S(1)} %reshape.22, bf16[224,3584]{1,0:T(8,128)(2,1)S(1)} %copy-done.1, f32[224]{0:T(256)S(1)} %add_sqrt_fusion, f32[224]{0:T(256)S(1)} %get-tuple-element.8), kind=kOutput, calls=%fused_computation.1 | convolution fusion | flops 55394304 | bytes 3456768 | tf_op jit(solution)/shard_map/dot_general | solution.py:45
  136.9 0.0 copy-done.3
  136.9 24.8 %all-reduce.1 = (f32[3584]{0:T(1024)}, f32[]{:T(128)}) all-reduce(f32[3584]{0:T(1024)S(1)} %get-tuple-element.6, f32[]{:T(128)} %get-tuple-element.5), channel_id=1, replica_groups=mesh['section'=4,'tensor'=8] {'tensor'}, use_global_device_ids=true, to_apply=%region_5.6 | all-reduce | flops 3585 | bytes 28680 | tf_op jit(solution)/shard_map/psum | solution.py:41
  (2 shorter events, 0.0 us)
Async XLA Ops:
  7.2 35.8 %copy-start = (bf16[224,3584]{1,0:T(8,128)(2,1)S(1)}, bf16[224,3584]{1,0:T(8,128)(2,1)}, u32[]{:S(2)}) copy-start(bf16[224,3584]{1,0:T(8,128)(2,1)} %param.6) | copy-start | bytes 4816900
  7.2 30.4 %copy-start.2 = (bf16[4,3584]{1,0:T(4,128)(2,1)S(1)}, bf16[4,3584]{1,0:T(4,128)(2,1)}, u32[]{:S(2)}) copy-start(bf16[4,3584]{1,0:T(4,128)(2,1)} %param.5) | copy-start | bytes 86020
  7.2 35.7 %copy-start.5 = (f32[224]{0:T(256)S(1)}, f32[224]{0:T(256)}, u32[]{:S(2)}) copy-start(f32[224]{0:T(256)} %param.7) | copy-start | bytes 2692
  7.2 95.0 %all-reduce.4.cloned.1.call-start = ((), (), s32[]{:S(2)}) async-start(), calls=%async_computation | async-start | bytes 917504
  7.2 5.2 %collective-permute-start = (bf16[4,3584]{1,0:T(4,128)(2,1)}, bf16[4,3584]{1,0:T(4,128)(2,1)S(1)}, u32[]{:S(2)}, u32[]{:S(2)}) collective-permute-start(bf16[4,3584]{1,0:T(4,128)(2,1)} %param.5), channel_id=1, source_target_pairs={{0,1},{1,2},{2,3},{3,4},{4,5},{5,6},{6,7},{7,0},{8,9},{9,10},{10,1... | collective-permute-start | bytes 86024 | tf_op jit(solution)/shard_map/ppermute | solution.py:15
  12.4 4.2 %collective-permute-start.1 = (bf16[4,3584]{1,0:T(4,128)(2,1)S(1)}, bf16[4,3584]{1,0:T(4,128)(2,1)S(1)}, u32[]{:S(2)}, u32[]{:S(2)}) collective-permute-start(bf16[4,3584]{1,0:T(4,128)(2,1)S(1)} %collective-permute-done), channel_id=1, source_target_pairs={{0,1},{1,2},{2,3},{3,4},{4,5},{5,6},{6,7},{7,0},{8,9},{9,10},{10,1... | collective-permute-start | bytes 86024 | tf_op jit(solution)/shard_map/ppermute | solution.py:15
  16.6 4.2 %collective-permute-start.2 = (bf16[4,3584]{1,0:T(4,128)(2,1)S(1)}, bf16[4,3584]{1,0:T(4,128)(2,1)S(1)}, u32[]{:S(2)}, u32[]{:S(2)}) collective-permute-start(bf16[4,3584]{1,0:T(4,128)(2,1)S(1)} %collective-permute-done.1), channel_id=1, source_target_pairs={{0,1},{1,2},{2,3},{3,4},{4,5},{5,6},{6,7},{7,0},{8,9},{9,10},{10,1... | collective-permute-start | bytes 86024 | tf_op jit(solution)/shard_map/ppermute | solution.py:15
  20.8 4.2 %collective-permute-start.3 = (bf16[4,3584]{1,0:T(4,128)(2,1)S(1)}, bf16[4,3584]{1,0:T(4,128)(2,1)S(1)}, u32[]{:S(2)}, u32[]{:S(2)}) collective-permute-start(bf16[4,3584]{1,0:T(4,128)(2,1)S(1)} %collective-permute-done.2), channel_id=1, source_target_pairs={{0,1},{1,2},{2,3},{3,4},{4,5},{5,6},{6,7},{7,0},{8,9},{9,10},{10,1... | collective-permute-start | bytes 86024 | tf_op jit(solution)/shard_map/ppermute | solution.py:15
  25.0 4.2 %collective-permute-start.4 = (bf16[4,3584]{1,0:T(4,128)(2,1)S(1)}, bf16[4,3584]{1,0:T(4,128)(2,1)S(1)}, u32[]{:S(2)}, u32[]{:S(2)}) collective-permute-start(bf16[4,3584]{1,0:T(4,128)(2,1)S(1)} %collective-permute-done.3), channel_id=1, source_target_pairs={{0,1},{1,2},{2,3},{3,4},{4,5},{5,6},{6,7},{7,0},{8,9},{9,10},{10,1... | collective-permute-start | bytes 86024 | tf_op jit(solution)/shard_map/ppermute | solution.py:15
  29.2 4.2 %collective-permute-start.5 = (bf16[4,3584]{1,0:T(4,128)(2,1)S(1)}, bf16[4,3584]{1,0:T(4,128)(2,1)S(1)}, u32[]{:S(2)}, u32[]{:S(2)}) collective-permute-start(bf16[4,3584]{1,0:T(4,128)(2,1)S(1)} %collective-permute-done.4), channel_id=1, source_target_pairs={{0,1},{1,2},{2,3},{3,4},{4,5},{5,6},{6,7},{7,0},{8,9},{9,10},{10,1... | collective-permute-start | bytes 86024 | tf_op jit(solution)/shard_map/ppermute | solution.py:15
  31.0 14.1 %copy-start.1 = (bf16[224,3584]{1,0:T(8,128)(2,1)S(1)}, bf16[224,3584]{1,0:T(8,128)(2,1)}, u32[]{:S(2)}) copy-start(bf16[224,3584]{1,0:T(8,128)(2,1)} %param.8) | copy-start | bytes 4816900
  33.4 4.2 %collective-permute-start.6 = (bf16[4,3584]{1,0:T(4,128)(2,1)S(1)}, bf16[4,3584]{1,0:T(4,128)(2,1)S(1)}, u32[]{:S(2)}, u32[]{:S(2)}) collective-permute-start(bf16[4,3584]{1,0:T(4,128)(2,1)S(1)} %collective-permute-done.5), channel_id=1, source_target_pairs={{0,1},{1,2},{2,3},{3,4},{4,5},{5,6},{6,7},{7,0},{8,9},{9,10},{10,1... | collective-permute-start | bytes 86024 | tf_op jit(solution)/shard_map/ppermute | solution.py:15
  45.1 1.2 copy-start.6
  45.1 77.6 %copy-start.4 = (f32[3584]{0:T(1024)S(1)}, f32[3584]{0:T(1024)}, u32[]{:S(2)}) copy-start(f32[3584]{0:T(1024)} %param.9) | copy-start | bytes 43012
  123.3 13.6 %copy-start.3 = (f32[4,3584]{1,0:T(4,128)}, f32[4,3584]{1,0:T(4,128)S(1)}, u32[]{:S(2)}) copy-start(f32[4,3584]{1,0:T(4,128)S(1)} %get-tuple-element.11) | copy-start | bytes 172036
Sparse Core Ops, SparseCore 0:
  46.4 55.7 all-reduce.3
